TPU v7x, 512 devices: a whole 4x8x8 slice. The times are simulated.
512 devices in a mesh: rows: 64 (over y, x, core), cols: 8 (over z).
Axes of the slice: x: 4, y: 8, z: 8, core: 2. Of those that a mesh axis runs over, the one named last changes fastest.
Arguments:
- fact_cells: bfloat16 [3072, 32, 512], P('rows', 'cols'), may hold values from -6 to 6
- gain_col: float32 [512], replicated, may hold values from 0.1 to 1.9
- w_qkv: bfloat16 [512, 1536], replicated, may hold values from -0.25 to 0.25
- w_col_out: bfloat16 [512, 512], replicated, may hold values from -0.25 to 0.25
- gain_tile: float32 [512], replicated, may hold values from 0.1 to 1.9
- w_query: bfloat16 [512, 512], replicated, may hold values from -0.25 to 0.25
- w_tile_out: bfloat16 [512, 512], replicated, may hold values from -0.25 to 0.25
- tile_kv: bfloat16 [256, 128, 8, 128], P('rows', None, 'cols'), may hold values from -70 to 70
- tile_ids: int32 [64, 48], P('rows'), may hold values from -1 to 255, as said below
- key_mask: int32 [3072, 48], P('rows'), may hold values from 0 to 1, as said below
Outputs:
- layer_out: bfloat16 [3072, 32, 512], P('rows', 'cols')
Inputs may be any that keep to these rules, and one draw needn't show every extreme that they name: `tile_ids`: tile t is held by index t // 4 of rows. In every block the first slots, 36 of them or more, hold distinct tile ids and the rest hold -1; some block fills all 48 slots. The listed tiles of one block are held by distinct indices of rows. `key_mask`: 0 wherever the row's block holds -1 in that slot; 1 in slot 0 of every row.
All inputs are finite; a program needn't handle non-finite values.
Results may differ from a plain program's by a relative error of at most 0.023.
The roundings to bfloat16 on the way count: a program that leaves them out, or rounds other values in their place, can miss the bound.
Values may be sent and summed in bfloat16 or wider, within the bound.
A program may use at most 64 MiB of HBM per device.

v0:
```python
import jax
import jax.numpy as jnp
from jax import lax
from jax.sharding import PartitionSpec as P


def rms_scale(values, gain_vec):
    mean_sq = jnp.mean(values * values, axis=-1, keepdims=True)
    return values * lax.rsqrt(mean_sq + 1e-05) * gain_vec


def soft_weights(scores, axes):
    row_top = jnp.max(scores, axis=axes, keepdims=True)
    expo_vals = jnp.exp(scores - row_top)
    return (expo_vals / jnp.sum(expo_vals, axis=axes, keepdims=True)).astype(jnp.bfloat16)


def column_attend(queries, keyvals, head_size):
    key_part = keyvals[..., :head_size]
    val_part = keyvals[..., head_size:]
    scores = jnp.einsum(
        "rchd,rkhd->rhck", queries, key_part, preferred_element_type=jnp.float32
    ) * head_size ** (-0.5)
    col_weights = soft_weights(scores, (3,))
    return jnp.einsum(
        "rhck,rkhd->rchd", col_weights, val_part, preferred_element_type=jnp.float32
    ).astype(jnp.bfloat16)


def tile_attend(queries, fetched, key_mask, head_size):
    key_part = fetched[..., :head_size]
    val_part = fetched[..., head_size:]
    row_count, col_count, head_count = queries.shape[:3]
    q_blocks = queries.reshape(row_count // 4, 4, col_count, head_count, head_size)
    m_blocks = key_mask.reshape(row_count // 4, 4, key_mask.shape[1])

    def one_block(block_pair):
        block_q, block_m = block_pair
        scores = jnp.einsum(
            "rchd,tkhd->rchtk", block_q, key_part, preferred_element_type=jnp.float32
        ) * head_size ** (-0.5)
        live_keys = (block_m > 0)[:, None, None, :, None]
        scores = jnp.where(live_keys, scores, -1e30)
        tile_weights = soft_weights(scores, (3, 4))
        return jnp.einsum(
            "rchtk,tkhd->rchd", tile_weights, val_part, preferred_element_type=jnp.float32
        ).astype(jnp.bfloat16)

    answer = lax.map(one_block, (q_blocks, m_blocks))
    return answer.reshape(row_count, col_count, head_count, head_size)


def fetch_all(tile_kv, tile_ids):
    gathered = lax.all_gather(tile_kv, "rows", axis=0, tiled=True)
    return jnp.take(gathered, jnp.maximum(tile_ids[0], 0), axis=0)


def project(normed, weight):
    return jnp.dot(normed.reshape(-1, weight.shape[0]), weight, preferred_element_type=jnp.float32)


def shards(
    fact_cells,
    gain_col,
    w_qkv,
    w_col_out,
    gain_tile,
    w_query,
    w_tile_out,
    tile_kv,
    tile_ids,
    key_mask,
):
    model_width = fact_cells.shape[2]
    head_size = tile_kv.shape[3] // 2
    heads_all = model_width // head_size
    fetched = fetch_all(tile_kv, tile_ids)
    row_count, col_local = (fact_cells.shape[0], fact_cells.shape[1])
    residual = fact_cells.astype(jnp.float32)
    normed = rms_scale(residual, gain_col).astype(jnp.bfloat16)
    packed = (
        project(normed, w_qkv)
        .astype(jnp.bfloat16)
        .reshape(row_count, col_local, 3, heads_all, head_size)
    )
    queries = packed[:, :, 0]
    keyvals = jnp.concatenate([packed[:, :, 1], packed[:, :, 2]], axis=-1)
    queries_h, keyvals_h = (
        lax.all_to_all(queries, "cols", split_axis=2, concat_axis=1, tiled=True),
        lax.all_to_all(keyvals, "cols", split_axis=2, concat_axis=1, tiled=True),
    )
    mixed_col = column_attend(queries_h, keyvals_h, head_size)
    mixed_back = lax.all_to_all(mixed_col, "cols", split_axis=1, concat_axis=2, tiled=True)
    residual = residual + project(mixed_back, w_col_out).reshape(residual.shape)
    normed2 = rms_scale(residual, gain_tile).astype(jnp.bfloat16)
    asked_q = (
        project(normed2, w_query)
        .astype(jnp.bfloat16)
        .reshape(row_count, col_local, heads_all, head_size)
    )
    asked_h = lax.all_to_all(asked_q, "cols", split_axis=2, concat_axis=1, tiled=True)
    answer = tile_attend(asked_h, fetched, key_mask, head_size)
    answer_back = lax.all_to_all(answer, "cols", split_axis=1, concat_axis=2, tiled=True)
    final_out = residual + project(answer_back, w_tile_out).reshape(residual.shape)
    return final_out.astype(jnp.bfloat16)


def solution(mesh):
    placed = (
        P("rows", "cols", None),
        P(),
        P(),
        P(),
        P(),
        P(),
        P(),
        P("rows", None, "cols", None),
        P("rows", None),
        P("rows", None),
    )
    return jax.shard_map(
        shards, mesh=mesh, in_specs=placed, out_specs=P("rows", "cols", None), check_vma=False
    )
```

profile of v0, /device:TPU:1, one launch (start us, length us, event | category | flops | bytes accessed | tf_op | source)
XLA Modules:
  0.0 197.9 jit_solution(1383678545264350636)
XLA Ops:
  7.3 1.1 fusion.30
  8.3 1.1 fusion.32
  11.1 1.0 reshape.174
  12.1 10.9 %all-to-all-start.1 = ((bf16[8,2,6144]{2,1,0:T(2,128)(2,1)}), bf16[8,2,6144]{2,1,0:T(2,128)(2,1)S(1)}, u32[]{:S(2)}, u32[]{:S(2)}) async-start(bf16[8,2,6144]{2,1,0:T(2,128)(2,1)} %reshape.174), calls=%async_computation.1 | async-start | bytes 393216 | tf_op jit(solution)/shard_map/all_to_all | solution.py:89
  23.4 1.3 pad_maximum_fusion
  24.7 7.1 %all-to-all-done.1 = bf16[8,2,6144]{2,1,0:T(2,128)(2,1)S(1)} async-done(((bf16[8,2,6144]{2,1,0:T(2,128)(2,1)}), bf16[8,2,6144]{2,1,0:T(2,128)(2,1)S(1)}, u32[]{:S(2)}, u32[]{:S(2)}) %all-to-all-start.1) | async-done | bytes 196640 | tf_op jit(solution)/shard_map/all_to_all | solution.py:89
  31.8 3.5 %all-to-all-start = ((bf16[48,4,8,128]{3,1,0,2:T(4,128)(2,1)}), bf16[48,4,8,128]{3,1,0,2:T(4,128)(2,1)S(1)}, u32[]{:S(2)}, u32[]{:S(2)}) async-start(bf16[48,4,8,128]{3,1,0,2:T(4,128)(2,1)} %pad_maximum_fusion), calls=%async_computation | async-start | bytes 786432 | tf_op jit(solution)/shard_map/all_to_all | solution.py:90
  35.9 11.1 %all-to-all-done = bf16[48,4,8,128]{3,1,0,2:T(4,128)(2,1)S(1)} async-done(((bf16[48,4,8,128]{3,1,0,2:T(4,128)(2,1)}), bf16[48,4,8,128]{3,1,0,2:T(4,128)(2,1)S(1)}, u32[]{:S(2)}, u32[]{:S(2)}) %all-to-all-start) | async-done | bytes 393248 | tf_op jit(solution)/shard_map/all_to_all | solution.py:90
  47.2 1.3 fusion.38
  48.5 1.6 fusion.26
  50.6 11.4 %all_to_all.78 = bf16[8,2,6144]{2,1,0:T(2,128)(2,1)S(1)} all-to-all(bf16[8,2,6144]{2,1,0:T(2,128)(2,1)S(1)} %reshape.176), channel_id=1, replica_groups=mesh['rows'=64,'cols'=8] {'cols'}, dimensions={0} | all-to-all | bytes 393216 | tf_op jit(solution)/shard_map/all_to_all | solution.py:93
  63.5 1.3 convolution_convert_fusion.2
  65.2 1.0 reshape.178
  66.2 3.6 %all-to-all-start.3 = ((bf16[8,2,6144]{2,1,0:T(2,128)(2,1)}), bf16[8,2,6144]{2,1,0:T(2,128)(2,1)S(1)}, u32[]{:S(2)}, u32[]{:S(2)}) async-start(bf16[8,2,6144]{2,1,0:T(2,128)(2,1)} %reshape.178), calls=%async_computation.3 | async-start | bytes 393216 | tf_op jit(solution)/shard_map/all_to_all | solution.py:101
  69.9 8.3 %all-to-all-done.3 = bf16[8,2,6144]{2,1,0:T(2,128)(2,1)S(1)} async-done(((bf16[8,2,6144]{2,1,0:T(2,128)(2,1)}), bf16[8,2,6144]{2,1,0:T(2,128)(2,1)S(1)}, u32[]{:S(2)}, u32[]{:S(2)}) %all-to-all-start.3) | async-done | bytes 196640 | tf_op jit(solution)/shard_map/all_to_all | solution.py:101
  79.5 25.3 %all-gather.2.cloned.1.call-done = bf16[256,128,1,128]{3,1,2,0:T(8,128)(2,1)} async-done(((bf16[4,128,1,128]{3,1,2,0:T(8,128)(2,1)}), bf16[256,128,1,128]{3,1,2,0:T(8,128)(2,1)}) %all-gather.2.cloned.1.call-update) | async-done | bytes 8388624 | tf_op jit(solution)/shard_map/all_gather | solution.py:54
  104.8 4.2 %gather_fusion = bf16[48,128,128]{2,1,0:T(8,128)(2,1)S(1)} fusion(bf16[256,128,128]{2,1,0:T(8,128)(2,1)} %bitcast.194, s32[1024]{0:T(1024)S(1)} %pad_clamp_fusion), kind=kCustom, calls=%fused_computation | custom fusion | bytes 3145920 | tf_op jit(solution)/shard_map/jit(_take)/gather | solution.py:55
  109.3 1.9 fusion.36
  111.1 1.4 copy.66
  112.6 1.7 copy.65
  114.3 56.9 %while.10 = (s32[]{:T(128)}, bf16[12,4,32,1,64]{4,1,0,2,3:T(4,128)(2,1)}, s32[12,4,48]{2,1,0:T(4,128)}, bf16[12,4,32,1,64]{4,2,1,3,0:T(8,128)(2,1)}, bf16[48,128...) while((s32[]{:T(128)}, bf16[12,4,32,1,64]{4,1,0,2,3:T(4,128)(2,1)}, ...), condition=%wide.region_7.8_spmd, body=%wide.region_4.0_spmd.sunk | while | flops 210771904 | bytes 14258301 | solution.py:49
  115.0 1.5 fusion.56
  116.5 0.9 fusion.57
  117.5 1.0 fusion.58
  119.8 1.5 fusion.56
  122.2 1.0 fusion.58
  124.5 1.5 fusion.56
  126.9 1.0 fusion.58
  129.2 1.5 fusion.56
  131.7 1.0 fusion.58
  134.0 1.5 fusion.56
  136.4 1.0 fusion.58
  138.7 1.5 fusion.56
  141.2 1.0 fusion.58
  143.4 1.5 fusion.56
  145.9 1.0 fusion.58
  148.2 1.5 fusion.56
  150.7 1.0 fusion.58
  152.9 1.5 fusion.56
  155.4 1.0 fusion.58
  157.7 1.5 fusion.56
  160.1 1.0 fusion.58
  162.4 1.5 fusion.56
  164.9 1.0 fusion.58
  167.2 1.5 fusion.56
  169.6 1.0 fusion.58
  171.2 1.4 reshape.180
  172.6 16.5 %all_to_all.79 = bf16[8,2,6144]{2,1,0:T(2,128)(2,1)S(1)} all-to-all(bf16[8,2,6144]{2,1,0:T(2,128)(2,1)S(1)} %reshape.180), channel_id=1, replica_groups=mesh['rows'=64,'cols'=8] {'cols'}, dimensions={0} | all-to-all | bytes 393216 | tf_op jit(solution)/shard_map/all_to_all | solution.py:103
  (110 shorter events, 35.7 us)
Async XLA Ops:
  6.5 3.1 %copy-start = (bf16[512,1536]{1,0:T(8,128)(2,1)S(1)}, bf16[512,1536]{1,0:T(8,128)(2,1)}, u32[]{:S(2)}) copy-start(bf16[512,1536]{1,0:T(8,128)(2,1)} %param.14) | copy-start | bytes 4718596
  6.5 98.3 %all-gather.2.cloned.1.call-start = ((), (), s32[]{:S(2)}) async-start(), calls=%async_computation.5 | async-start | bytes 8519680 | tf_op jit(solution)/shard_map/all_gather | solution.py:54
  12.1 19.7 %all-to-all-start.1 = ((bf16[8,2,6144]{2,1,0:T(2,128)(2,1)}), bf16[8,2,6144]{2,1,0:T(2,128)(2,1)S(1)}, u32[]{:S(2)}, u32[]{:S(2)}) async-start(bf16[8,2,6144]{2,1,0:T(2,128)(2,1)} %reshape.174), calls=%async_computation.1 | async-start | bytes 393216 | tf_op jit(solution)/shard_map/all_to_all | solution.py:89
  31.8 15.2 %all-to-all-start = ((bf16[48,4,8,128]{3,1,0,2:T(4,128)(2,1)}), bf16[48,4,8,128]{3,1,0,2:T(4,128)(2,1)S(1)}, u32[]{:S(2)}, u32[]{:S(2)}) async-start(bf16[48,4,8,128]{3,1,0,2:T(4,128)(2,1)} %pad_maximum_fusion), calls=%async_computation | async-start | bytes 786432 | tf_op jit(solution)/shard_map/all_to_all | solution.py:90
  48.5 14.3 %copy-start.1 = (bf16[48,4,512]{2,1,0:T(4,128)(2,1)S(1)}, bf16[48,4,512]{2,1,0:T(4,128)(2,1)}, u32[]{:S(2)}) copy-start(bf16[48,4,512]{2,1,0:T(4,128)(2,1)} %param.12) | copy-start | bytes 589828
  48.5 14.3 %copy-start.3 = (bf16[512,512]{1,0:T(8,128)(2,1)S(1)}, bf16[512,512]{1,0:T(8,128)(2,1)}, u32[]{:S(2)}) copy-start(bf16[512,512]{1,0:T(8,128)(2,1)} %param.15) | copy-start | bytes 1572868
  50.1 13.1 %copy-start.5 = (f32[512]{0:T(512)S(1)}, f32[512]{0:T(512)}, u32[]{:S(2)}) copy-start(f32[512]{0:T(512)} %param.16) | copy-start | bytes 6148
  62.5 7.3 %copy-start.6 = (s32[1,48]{1,0:T(1,128)S(1)}, s32[1,48]{1,0:T(1,128)}, u32[]{:S(2)}) copy-start(s32[1,48]{1,0:T(1,128)} %param.20) | copy-start | bytes 580
  66.2 11.9 %all-to-all-start.3 = ((bf16[8,2,6144]{2,1,0:T(2,128)(2,1)}), bf16[8,2,6144]{2,1,0:T(2,128)(2,1)S(1)}, u32[]{:S(2)}, u32[]{:S(2)}) async-start(bf16[8,2,6144]{2,1,0:T(2,128)(2,1)} %reshape.178), calls=%async_computation.3 | async-start | bytes 393216 | tf_op jit(solution)/shard_map/all_to_all | solution.py:101
  115.0 2.4 %copy-start.2 = (bf16[48,128,1,64]{1,3,0,2:T(8,128)(2,1)S(1)}, bf16[48,128,1,64]{1,3,0,2:T(8,128)(2,1)}, u32[]{:S(2)}) copy-start(bf16[48,128,1,64]{1,3,0,2:T(8,128)(2,1)} %get-tuple-element.141) | copy-start | bytes 2359300 | tf_op jit(solution)/shard_map/while
  119.8 2.4 %copy-start.2 = (bf16[48,128,1,64]{1,3,0,2:T(8,128)(2,1)S(1)}, bf16[48,128,1,64]{1,3,0,2:T(8,128)(2,1)}, u32[]{:S(2)}) copy-start(bf16[48,128,1,64]{1,3,0,2:T(8,128)(2,1)} %get-tuple-element.141) | copy-start | bytes 2359300 | tf_op jit(solution)/shard_map/while
  124.5 2.4 %copy-start.2 = (bf16[48,128,1,64]{1,3,0,2:T(8,128)(2,1)S(1)}, bf16[48,128,1,64]{1,3,0,2:T(8,128)(2,1)}, u32[]{:S(2)}) copy-start(bf16[48,128,1,64]{1,3,0,2:T(8,128)(2,1)} %get-tuple-element.141) | copy-start | bytes 2359300 | tf_op jit(solution)/shard_map/while
  129.2 2.4 %copy-start.2 = (bf16[48,128,1,64]{1,3,0,2:T(8,128)(2,1)S(1)}, bf16[48,128,1,64]{1,3,0,2:T(8,128)(2,1)}, u32[]{:S(2)}) copy-start(bf16[48,128,1,64]{1,3,0,2:T(8,128)(2,1)} %get-tuple-element.141) | copy-start | bytes 2359300 | tf_op jit(solution)/shard_map/while
  134.0 2.4 %copy-start.2 = (bf16[48,128,1,64]{1,3,0,2:T(8,128)(2,1)S(1)}, bf16[48,128,1,64]{1,3,0,2:T(8,128)(2,1)}, u32[]{:S(2)}) copy-start(bf16[48,128,1,64]{1,3,0,2:T(8,128)(2,1)} %get-tuple-element.141) | copy-start | bytes 2359300 | tf_op jit(solution)/shard_map/while
  138.7 2.4 %copy-start.2 = (bf16[48,128,1,64]{1,3,0,2:T(8,128)(2,1)S(1)}, bf16[48,128,1,64]{1,3,0,2:T(8,128)(2,1)}, u32[]{:S(2)}) copy-start(bf16[48,128,1,64]{1,3,0,2:T(8,128)(2,1)} %get-tuple-element.141) | copy-start | bytes 2359300 | tf_op jit(solution)/shard_map/while
  143.4 2.4 %copy-start.2 = (bf16[48,128,1,64]{1,3,0,2:T(8,128)(2,1)S(1)}, bf16[48,128,1,64]{1,3,0,2:T(8,128)(2,1)}, u32[]{:S(2)}) copy-start(bf16[48,128,1,64]{1,3,0,2:T(8,128)(2,1)} %get-tuple-element.141) | copy-start | bytes 2359300 | tf_op jit(solution)/shard_map/while
  148.2 2.4 %copy-start.2 = (bf16[48,128,1,64]{1,3,0,2:T(8,128)(2,1)S(1)}, bf16[48,128,1,64]{1,3,0,2:T(8,128)(2,1)}, u32[]{:S(2)}) copy-start(bf16[48,128,1,64]{1,3,0,2:T(8,128)(2,1)} %get-tuple-element.141) | copy-start | bytes 2359300 | tf_op jit(solution)/shard_map/while
  152.9 2.4 %copy-start.2 = (bf16[48,128,1,64]{1,3,0,2:T(8,128)(2,1)S(1)}, bf16[48,128,1,64]{1,3,0,2:T(8,128)(2,1)}, u32[]{:S(2)}) copy-start(bf16[48,128,1,64]{1,3,0,2:T(8,128)(2,1)} %get-tuple-element.141) | copy-start | bytes 2359300 | tf_op jit(solution)/shard_map/while
  157.7 2.4 %copy-start.2 = (bf16[48,128,1,64]{1,3,0,2:T(8,128)(2,1)S(1)}, bf16[48,128,1,64]{1,3,0,2:T(8,128)(2,1)}, u32[]{:S(2)}) copy-start(bf16[48,128,1,64]{1,3,0,2:T(8,128)(2,1)} %get-tuple-element.141) | copy-start | bytes 2359300 | tf_op jit(solution)/shard_map/while
  162.4 2.4 %copy-start.2 = (bf16[48,128,1,64]{1,3,0,2:T(8,128)(2,1)S(1)}, bf16[48,128,1,64]{1,3,0,2:T(8,128)(2,1)}, u32[]{:S(2)}) copy-start(bf16[48,128,1,64]{1,3,0,2:T(8,128)(2,1)} %get-tuple-element.141) | copy-start | bytes 2359300 | tf_op jit(solution)/shard_map/while
  167.2 2.4 %copy-start.2 = (bf16[48,128,1,64]{1,3,0,2:T(8,128)(2,1)S(1)}, bf16[48,128,1,64]{1,3,0,2:T(8,128)(2,1)}, u32[]{:S(2)}) copy-start(bf16[48,128,1,64]{1,3,0,2:T(8,128)(2,1)} %get-tuple-element.141) | copy-start | bytes 2359300 | tf_op jit(solution)/shard_map/while
  171.2 18.7 %copy-start.4 = (bf16[512,512]{1,0:T(8,128)(2,1)S(1)}, bf16[512,512]{1,0:T(8,128)(2,1)}, u32[]{:S(2)}) copy-start(bf16[512,512]{1,0:T(8,128)(2,1)} %param.18) | copy-start | bytes 1572868
Sparse Core Ops, SparseCore 0:
  10.7 94.0 all-gather.1
where the time goes:
time: 200 us; the launch traced here: 198 us
  waiting for transfers between devices  52.6 us (26%)
  matrix products  34.6 us (17%)
  blocking collectives  27.9 us (14%)
  local copies, waits for them, and re-layouts  27.5 us (14%)
  other arithmetic  23.4 us (12%)
  starting transfers between devices  17.9 us (9%)
  between operations  13.8 us (7%)
    all_gather x1, waiting for transfers between devices, fetch_all(): gathered = lax.all_gather(tile_kv, 'rows', axis=0, tiled=True)  25.3 us
    dot_general x12, matrix products, one_block(): jnp.einsum('rchd,tkhd->rchtk', block_q, key_part, preferred_element_type=...  17.6 us
    all_to_all x1, blocking collectives, shards(): lax.all_to_all(answer, 'cols', split_axis=1, concat_axis=2, tiled=True)  16.5 us
    dot_general x12, matrix products, one_block(): jnp.einsum('rchtk,tkhd->rchd', tile_weights, val_part, preferred_element_...  11.6 us
    reduce_sum x12, other arithmetic, soft_weights(): jnp.sum(expo_vals, axis=axes, keepdims=True)  11.4 us
    all_to_all x1, blocking collectives, shards(): lax.all_to_all(mixed_col, 'cols', split_axis=1, concat_axis=2, tiled=True)  11.4 us
    all_to_all x1, waiting for transfers between devices, shards(): lax.all_to_all(keyvals, 'cols', split_axis=2, concat_axis=1, tiled=True)  11.1 us
    all_to_all x1, starting transfers between devices, shards(): lax.all_to_all(queries, 'cols', split_axis=2, concat_axis=1, tiled=True)  10.9 us
  transfers between devices with their start and end apart: 4, of which 4 were waited for; matrix products, arithmetic and copies ran while one was open for 8% of the time, Pallas kernels for 0%

commit v1 on v0

v1 whole, which is shorter than its diff:
```python
import functools
import math

import jax
import jax.numpy as jnp
from jax import lax
from jax.experimental import pallas as pl
from jax.experimental.pallas import tpu as pltpu
from jax.sharding import PartitionSpec as P

F32, BF = jnp.float32, jnp.bfloat16
MESH = pl.DeviceIdType.MESH
NT = (((1,), (1,)), ((), ()))
ZN = 8
GROUP = 24
CELLS = ZN * GROUP
D = 512
PLANE = 8
STEPS = ((0, 0), (1, 1), (-1, 5), (2, 2), (-2, 6), (3, 3), (-3, 7), (4, 4))


def rms(values, gain):
    mean_sq = jnp.mean(values * values, axis=-1, keepdims=True)
    return (values * lax.rsqrt(mean_sq + 1e-05) * gain).astype(BF)


def row_of(shape, dim):
    return (lax.broadcasted_iota(jnp.int32, shape, dim) % GROUP) >> 2


def layer_kernel(
    rows_n,
    maxt,
    ids_ref,
    mask_ref,
    fact_ref,
    gain_col_ref,
    gain_tile_ref,
    tile_ref,
    w_qkv_hbm,
    w_col_hbm,
    w_query_hbm,
    w_out_hbm,
    out_ref,
    xin,
    packed_buf,
    delta_send,
    delta_buf,
    q_send,
    q_buf,
    o_send,
    a_buf,
    y1,
    y2,
    y3,
    y4,
    y5,
    y6,
    y7,
    x_send,
    kv_buf,
    k_all,
    v_all,
    my_list,
    lists,
    lists_s,
    w_qkv,
    w_col,
    w_query,
    w_pad,
    w_sem,
    list_sem,
    cell_ss,
    cell_rs,
    list_ss,
    list_rs,
    delta_ss,
    delta_rs,
    q_ss,
    q_rs,
    o_ss,
    o_rs,
    y_ss,
    y_rs,
    x_ss,
    x_rs,
):
    row = lax.axis_index("rows")
    me = lax.axis_index("cols")
    seat = lax.rem(row, PLANE)
    base = row - seat

    def at_z(k):
        return lax.rem(me + k, ZN)

    def at_seat(d):
        return base + lax.rem(seat + d, PLANE)

    def at_y(dy):
        return lax.rem(row + dy * PLANE + rows_n, rows_n)

    def to_z(src, dst, ss, rs, k):
        return pltpu.make_async_remote_copy(
            src, dst, ss, rs, device_id=(row, at_z(k)), device_id_type=MESH
        )

    def to_row(src, dst, ss, rs, r):
        return pltpu.make_async_remote_copy(src, dst, ss, rs, device_id=(r, me), device_id_type=MESH)

    w_copies = [
        pltpu.make_async_copy(w_qkv_hbm, w_qkv, w_sem.at[0]),
        pltpu.make_async_copy(w_col_hbm, w_col, w_sem.at[1]),
        pltpu.make_async_copy(w_query_hbm, w_query, w_sem.at[2]),
    ] + [
        pltpu.make_async_copy(
            w_out_hbm.at[pl.ds(64 * h, 64)], w_pad.at[pl.ds(128 * h + 64, 64)], w_sem.at[3 + h]
        )
        for h in range(ZN)
    ]
    for copy in w_copies:
        copy.start()

    barrier = pltpu.get_barrier_semaphore()

    @pl.loop(1, ZN)
    def _(k):
        pl.semaphore_signal(barrier, inc=1, device_id=(row, at_z(k)), device_id_type=MESH)
        pl.semaphore_signal(barrier, inc=1, device_id=(at_seat(k), me), device_id_type=MESH)

    for dy in (1, -1):
        pl.semaphore_signal(barrier, inc=1, device_id=(at_y(dy), me), device_id_type=MESH)

    lane8 = lax.broadcasted_iota(jnp.int32, (8, 128), 1)
    picks = jnp.zeros((8, 128), jnp.int32)
    for j in range(maxt):
        slot_id = ids_ref[0, j]
        picks = jnp.where(lane8 == (slot_id >> 2), slot_id & 3, picks)
    my_list[...] = picks
    lists[0] = picks
    for h in range(ZN):
        w_pad[pl.ds(128 * h, 64), :] = jnp.zeros((64, D), BF)

    pl.semaphore_wait(barrier, 16)

    @pl.loop(1, ZN)
    def _(k):
        to_z(fact_ref.at[at_z(k)], xin.at[me], cell_ss.at[k], cell_rs.at[k], k).start()
        to_row(my_list, lists.at[k], list_ss.at[k], list_rs.at[k], at_seat(k)).start()

    y_bufs = (None, y1, y2, y3, y4, y5, y6, y7)
    y_copies = []

    def y_forward(src, number, sign):
        copy = to_row(
            src,
            y_bufs[number + 1 if sign > 0 else number - 4 + 5],
            y_ss.at[number],
            y_rs.at[number],
            at_y(sign),
        )
        copy.start()
        y_copies.append(copy)

    y_forward(tile_ref, 0, 1)
    y_forward(tile_ref, 4, -1)
    xin[me] = fact_ref[me]

    @pl.loop(1, PLANE)
    def _(k):
        to_row(my_list, lists.at[k], list_ss.at[k], list_rs.at[k], at_seat(k)).wait()

    list_copy = pltpu.make_async_copy(lists, lists_s, list_sem)
    list_copy.start()
    list_copy.wait()

    def x_copy(s, d, owner):
        return to_row(
            x_send.at[s, d], kv_buf.at[owner], x_ss.at[s, d], x_rs.at[s, d], at_seat(d)
        )

    def hand_out(s, dy, src):
        owner = at_y(-dy)
        kv_buf[owner] = src[lists_s[0, 0, owner]]

        @pl.loop(1, PLANE)
        def _(d):
            x_send[s, d] = src[lists_s[PLANE - d, 0, owner]]
            x_copy(s, d, owner).start()

    def relay(s):
        dy, number = STEPS[s]
        buf = y_bufs[number]
        sem = number - 1
        to_row(buf, buf, y_ss.at[sem], y_rs.at[sem], at_y(1)).wait_recv()
        if dy > 0 and dy < 4:
            y_forward(buf, number, 1)
        if dy < 0 and dy > -3:
            y_forward(buf, number, -1)
        hand_out(s, dy, buf)

    hand_out(0, 0, tile_ref)

    @pl.loop(1, ZN)
    def _(k):
        to_z(fact_ref.at[at_z(k)], xin.at[me], cell_ss.at[k], cell_rs.at[k], k).wait()

    x = xin[...].astype(F32).reshape(CELLS, D)
    normed = rms(x, gain_col_ref[...])
    w_copies[0].wait()
    packed_buf[...] = jnp.dot(normed, w_qkv[...], preferred_element_type=F32).astype(BF)
    relay(1)
    relay(2)

    same_row = row_of((CELLS, CELLS), 0) == row_of((CELLS, CELLS), 1)
    low = lax.broadcasted_iota(jnp.int32, (CELLS, 128), 1) < 64
    mixed = []
    for pair in range(4):
        q2 = packed_buf[:, pl.ds(128 * pair, 128)]
        k2 = packed_buf[:, pl.ds(D + 128 * pair, 128)]
        v2 = packed_buf[:, pl.ds(2 * D + 128 * pair, 128)]
        parts = []
        for half in range(2):
            q1 = jnp.where(low if half == 0 else ~low, q2, jnp.zeros_like(q2))
            s = lax.dot_general(q1, k2, NT, preferred_element_type=F32) * 0.125
            s = jnp.where(same_row, s, -1e30)
            e = jnp.exp(s - jnp.max(s, axis=1, keepdims=True))
            w = (e / jnp.sum(e, axis=1, keepdims=True)).astype(BF)
            parts.append(jnp.dot(w, v2, preferred_element_type=F32))
        mixed.append(jnp.where(low, parts[0], parts[1]).astype(BF))
    mixed = jnp.concatenate(mixed, axis=1)
    w_copies[1].wait()
    delta = jnp.dot(mixed, w_col[...], preferred_element_type=F32)
    relay(3)
    relay(4)
    normed2 = rms(x + delta, gain_tile_ref[...])
    w_copies[2].wait()
    asked = jnp.dot(normed2, w_query[...], preferred_element_type=F32)
    asked = asked * (0.125 * math.log2(math.e))
    low96 = lax.broadcasted_iota(jnp.int32, (CELLS // 2, 128), 1) < 64
    for pair in range(4):
        top = asked[: CELLS // 2, 128 * pair : 128 * pair + 128]
        bot = asked[CELLS // 2 :, 128 * pair : 128 * pair + 128]
        q_send[2 * pair] = jnp.where(low96, top, pltpu.roll(bot, 64, 1)).astype(BF)
        q_send[2 * pair + 1] = jnp.where(low96, pltpu.roll(top, 64, 1), bot).astype(BF)
    delta_send[...] = delta.reshape(ZN, GROUP, D).astype(BF)
    q_buf[me] = q_send[me]
    delta_buf[me] = delta_send[me]

    def q_copy(k):
        return to_z(q_send.at[at_z(k)], q_buf.at[me], q_ss.at[k], q_rs.at[k], k)

    def delta_copy(k):
        return to_z(delta_send.at[at_z(k)], delta_buf.at[me], delta_ss.at[k], delta_rs.at[k], k)

    @pl.loop(1, ZN)
    def _(k):
        q_copy(k).start()

    @pl.loop(1, ZN)
    def _(k):
        delta_copy(k).start()

    for s in range(5, 8):
        relay(s)

    for s, (dy, _number) in enumerate(STEPS):

        @pl.loop(1, PLANE)
        def _(d):
            x_copy(s, d, at_y(-dy)).wait_recv()

    lane = lax.broadcasted_iota(jnp.int32, (128, 128), 1)

    @pl.loop(0, maxt)
    def _(j):
        kv = kv_buf[jnp.maximum(ids_ref[0, j], 0) >> 2].astype(F32)
        at = pl.ds(pl.multiple_of(j * 128, 128), 128)
        k_all[at, :] = jnp.where(lane < 64, kv, jnp.where(lane == 64 + j, 1.0, 0.0)).astype(BF)
        v_all[at, :] = jnp.where(lane < 64, jnp.where(lane == 0, 1.0, 0.0), kv).astype(BF)

    @pl.loop(1, ZN)
    def _(k):
        q_copy(k).wait()

    dead = jnp.where(mask_ref[...] > 0, 0.0, -1e30)
    rows_dev = dead.shape[0]
    dead = jnp.concatenate(
        [jnp.zeros((rows_dev, 64), F32), dead, jnp.zeros((rows_dev, 64 - maxt), F32)], axis=1
    ).astype(BF)

    def o_copy(z, k):
        return to_z(
            o_send.at[z, at_z(k)], a_buf.at[me, z], o_ss.at[z, k], o_rs.at[z, k], k
        )

    @pl.loop(0, ZN)
    def _(z):
        mine = z * 6 + row_of((CELLS, rows_dev), 0)
        pick = jnp.where(lax.broadcasted_iota(jnp.int32, (CELLS, rows_dev), 1) == mine, 1.0, 0.0)
        bias = jnp.dot(pick.astype(BF), dead, preferred_element_type=F32)
        q = q_buf[z].astype(F32)
        q = jnp.concatenate(
            [
                jnp.where(low96, q, bias[: CELLS // 2]),
                jnp.where(low96, pltpu.roll(q, 64, 1), bias[CELLS // 2 :]),
            ],
            axis=0,
        ).astype(BF)
        s = lax.dot_general(q, k_all[...], NT, preferred_element_type=F32)
        p = jnp.exp2(s - jnp.max(s, axis=1, keepdims=True)).astype(BF)
        o = jnp.dot(p, v_all[...], preferred_element_type=F32)
        o = o / o[:, 0:1]
        o_send[z] = o.reshape(ZN, GROUP, 128).astype(BF)
        a_buf[me, z] = o_send[z, me]

        @pl.loop(1, ZN)
        def _(k):
            o_copy(z, k).start()

    for copy in w_copies[3:]:
        copy.wait()

    @pl.loop(1, ZN)
    def _(k):
        delta_copy(k).wait()

    base_cells = fact_ref[...].astype(F32).reshape(CELLS, D) + delta_buf[...].astype(
        F32
    ).reshape(CELLS, D)

    @pl.loop(0, ZN)
    def _(z):
        @pl.loop(1, ZN)
        def _(k):
            o_copy(z, k).wait()

    answer = jnp.concatenate(
        [a_buf[h].astype(F32).reshape(CELLS, 128).astype(BF) for h in range(ZN)], axis=1
    )
    final = base_cells + jnp.dot(answer, w_pad[...], preferred_element_type=F32)
    out_ref[...] = final.reshape(ZN, GROUP, D).astype(BF)

    for copy in y_copies:
        copy.wait_send()
    for s, (dy, _number) in enumerate(STEPS):

        @pl.loop(1, PLANE)
        def _(d):
            x_copy(s, d, at_y(-dy)).wait_send()


def shards(
    fact_cells,
    gain_col,
    w_qkv,
    w_col_out,
    gain_tile,
    w_query,
    w_tile_out,
    tile_kv,
    tile_ids,
    key_mask,
    *,
    rows_n,
):
    maxt = tile_ids.shape[1]
    vmem = pl.BlockSpec(memory_space=pltpu.VMEM)
    smem = pl.BlockSpec(memory_space=pltpu.SMEM)
    anywhere = pl.BlockSpec(memory_space=pl.ANY)
    tiles = tile_kv.reshape(tile_kv.shape[0], tile_kv.shape[1], tile_kv.shape[3])
    dma = pltpu.SemaphoreType.DMA
    out = pl.pallas_call(
        functools.partial(layer_kernel, rows_n, maxt),
        out_shape=jax.ShapeDtypeStruct((ZN, GROUP, D), BF),
        in_specs=[smem, vmem, vmem, vmem, vmem, vmem] + [anywhere] * 4,
        out_specs=vmem,
        scratch_shapes=[
            pltpu.VMEM((ZN, GROUP, D), BF),
            pltpu.VMEM((CELLS, 3 * D), BF),
            pltpu.VMEM((ZN, GROUP, D), BF),
            pltpu.VMEM((ZN, GROUP, D), BF),
            pltpu.VMEM((ZN, CELLS // 2, 128), BF),
            pltpu.VMEM((ZN, CELLS // 2, 128), BF),
            pltpu.VMEM((ZN, ZN, GROUP, 128), BF),
            pltpu.VMEM((ZN, ZN, GROUP, 128), BF),
        ]
        + [pltpu.VMEM(tiles.shape, BF)] * 7
        + [
            pltpu.VMEM((8, PLANE, 128, 128), BF),
            pltpu.VMEM((rows_n, 128, 128), BF),
            pltpu.VMEM((maxt * 128, 128), BF),
            pltpu.VMEM((maxt * 128, 128), BF),
            pltpu.VMEM((8, 128), jnp.int32),
            pltpu.VMEM((PLANE, 8, 128), jnp.int32),
            pltpu.SMEM((PLANE, 8, 128), jnp.int32),
            pltpu.VMEM((D, 3 * D), BF),
            pltpu.VMEM((D, D), BF),
            pltpu.VMEM((D, D), BF),
            pltpu.VMEM((2 * D, D), BF),
            dma((3 + ZN,)),
            dma,
            dma((ZN,)),
            dma((ZN,)),
            dma((ZN,)),
            dma((ZN,)),
            dma((ZN,)),
            dma((ZN,)),
            dma((ZN,)),
            dma((ZN,)),
            dma((ZN, ZN)),
            dma((ZN, ZN)),
            dma((7,)),
            dma((7,)),
            dma((8, PLANE)),
            dma((8, PLANE)),
        ],
        compiler_params=pltpu.CompilerParams(
            collective_id=0, has_side_effects=True, vmem_limit_bytes=60 << 20
        ),
    )(
        tile_ids,
        key_mask,
        fact_cells.reshape(ZN, GROUP, D),
        gain_col.reshape(1, D),
        gain_tile.reshape(1, D),
        tiles,
        w_qkv,
        w_col_out,
        w_query,
        w_tile_out,
    )
    return out.reshape(fact_cells.shape)


def solution(mesh):
    placed = (
        P("rows", "cols", None),
        P(),
        P(),
        P(),
        P(),
        P(),
        P(),
        P("rows", None, "cols", None),
        P("rows", None),
        P("rows", None),
    )
    return jax.shard_map(
        functools.partial(shards, rows_n=mesh.shape["rows"]),
        mesh=mesh,
        in_specs=placed,
        out_specs=P("rows", "cols", None),
        check_vma=False,
    )
```

time: 200 us -> 71.1 us (0.36)
  Pallas kernels: 0 us -> 67.6 us
  waiting for transfers between devices: 52.6 us -> 0 us
  matrix products: 34.6 us -> 0 us
  blocking collectives: 27.9 us -> 0 us
  local copies, waits for them, and re-layouts: 27.5 us -> 3.31 us
  other arithmetic: 23.4 us -> 0 us
  starting transfers between devices: 17.9 us -> 0 us
  between operations: 13.8 us -> 0.01 us
    pallas_call x0 -> x1, Pallas kernels: none -> 67.6 us  [shards(): pl.pallas_call(functools.partial(layer_kernel, rows_n, maxt), out_shape=j...]
    dot_general x29 -> x0, matrix products: 33.2 us -> none  [the longest x12 17.6 us: one_block(): jnp.einsum('rchd,tkhd->rchtk', block_q, key_part, preferred_element_type=...]
    all_to_all x2 -> x0, blocking collectives: 27.9 us -> none  [the longest x1 16.5 us: shards(): lax.all_to_all(answer, 'cols', split_axis=1, concat_axis=2, tiled=True)]
    all_to_all x3 -> x0, waiting for transfers between devices: 26.6 us -> none  [the longest x1 11.1 us: shards(): lax.all_to_all(keyvals, 'cols', split_axis=2, concat_axis=1, tiled=True)]
    all_gather x1 -> x0, waiting for transfers between devices: 25.3 us -> none  [fetch_all(): gathered = lax.all_gather(tile_kv, 'rows', axis=0, tiled=True)]
    all_to_all x3 -> x0, starting transfers between devices: 17.9 us -> none  [the longest x1 10.9 us: shards(): lax.all_to_all(queries, 'cols', split_axis=2, concat_axis=1, tiled=True)]
    reduce_sum x13 -> x0, other arithmetic: 12.4 us -> none  [the longest x12 11.4 us: soft_weights(): jnp.sum(expo_vals, axis=axes, keepdims=True)]
    gt x12 -> x0, other arithmetic: 8.23 us -> none  [one_block(): live_keys = (block_m > 0)[:, None, None, :, None]]
  transfers between devices with their start and end apart: 4 -> 0, of which waited for: 4 -> 0; matrix products, arithmetic and copies ran while one was open for 8% -> 0% of each run, Pallas kernels for 0% -> 0%
where the time goes in v1:
time: 71.1 us; the launch traced here: 70.9 us
  Pallas kernels  67.6 us (95%)
  local copies, waits for them, and re-layouts  3.31 us (5%)
    pallas_call x1, Pallas kernels, shards(): pl.pallas_call(functools.partial(layer_kernel, rows_n, maxt), out_shape=j...  67.6 us
    reshape x1, local copies, waits for them, and re-layouts, shards(): return out.reshape(fact_cells.shape)  1.66 us
    reshape x1, local copies, waits for them, and re-layouts, shards(): fact_cells.reshape(ZN, GROUP, D)  1.65 us

profile of v1, /device:TPU:1, one launch (start us, length us, event | category | flops | bytes accessed | tf_op | source)
XLA Modules:
  0.0 70.9 jit_solution(9224534071138126473)
XLA Ops:
  0.0 1.7 %reshape.15.fact_ref = bf16[8,24,512]{2,1,0:T(8,128)(2,1)} reshape(bf16[48,4,512]{2,1,0:T(4,128)(2,1)} %param.10) | data formatting | bytes 393216 | tf_op jit(solution)/shard_map/reshape | solution.py:423
  1.7 67.6 %shard_map.100 = bf16[8,24,512]{2,1,0:T(8,128)(2,1)} custom-call(s32[1,48]{1,0:T(1,128)} %ids_ref.1, s32[48,48]{1,0:T(8,128)} %mask_ref.1, bf16[8,24,512]{2,1,0:T(8,128)(2,1)} %reshape.15.fact_ref, f32[1,512]{1,0:T(1,128)} %bitcast.4, f32[1,512]{1,0:T(1,128)} %bitcast.5, bf16[4,128,128]{2,1,0:T(8,128)(2,1)} %bitcast.3, bf16[512,1536]{1,0:T(8,128)(2,1)} %w_qkv_hbm.1, ...), custom_call_target="tpu_custom_call" | custom-call | tf_op jit(solution)/shard_map/pallas_call | solution.py:372
  69.3 1.7 %reshape.19 = bf16[48,4,512]{2,1,0:T(4,128)(2,1)} reshape(bf16[8,24,512]{2,1,0:T(8,128)(2,1)} %shard_map.100) | data formatting | bytes 393216 | tf_op jit(solution)/shard_map/reshape | solution.py:432

commit v2 on v0

v2 whole, which is shorter than its diff:
```python
import functools
import math

import jax
import jax.numpy as jnp
from jax import lax
from jax.experimental import pallas as pl
from jax.experimental.pallas import tpu as pltpu
from jax.sharding import PartitionSpec as P

F32, BF = jnp.float32, jnp.bfloat16
MESH = pl.DeviceIdType.MESH
NT = (((1,), (1,)), ((), ()))
ZN = 8
GROUP = 24
CELLS = ZN * GROUP
D = 512
EARLY_STEPS, EARLY = 6, 32
PARTS = ((0, 4), (4, 2))
LAST = 3
PLANE = 8
STEPS = ((0, 0), (1, 1), (-1, 5), (2, 2), (-2, 6), (3, 3), (-3, 7), (4, 4))


def rms(values, gain):
    mean_sq = jnp.mean(values * values, axis=-1, keepdims=True)
    return (values * lax.rsqrt(mean_sq + 1e-05) * gain).astype(BF)


def row_of(shape, dim, rows):
    return (lax.broadcasted_iota(jnp.int32, shape, dim) & (4 * rows - 1)) >> 2


def layer_kernel(
    rows_n,
    maxt,
    ids_ref,
    mask_hbm,
    fact_hbm,
    gain_col_hbm,
    gain_tile_hbm,
    tile_hbm,
    w_qkv_hbm,
    w_col_hbm,
    w_query_hbm,
    w_out_hbm,
    out_ref,
    mask_ref,
    fact_ref,
    gain_col_ref,
    gain_tile_ref,
    tile_ref,
    xin_a,
    xin_b,
    packed_a,
    packed_b,
    delta_send_a,
    delta_send_b,
    delta_buf_a,
    delta_buf_b,
    q_send_a,
    q_send_b,
    q_buf_a,
    q_buf_b,
    q_all,
    o_send_a,
    o_send_b,
    a_buf_a,
    a_buf_b,
    x_row,
    x_sib,
    y1,
    y2,
    y3,
    y4,
    y5,
    y6,
    y7,
    x_send,
    kv_early,
    kv_late,
    k_early,
    v_early,
    k_late,
    v_late,
    s_even,
    s_odd,
    o_first,
    m_first,
    o_even,
    my_list,
    lists,
    lists_s,
    w_qkv,
    w_col,
    w_query,
    w_twice,
    in_sem,
    w_sem,
    list_sem,
    y_sem,
    send_sem,
    recv_sem,
):
    row = lax.axis_index("rows")
    me = lax.axis_index("cols")
    seat = lax.rem(row, PLANE)
    base = row - seat

    def at_z(k):
        return lax.rem(me + k, ZN)

    def at_seat(d):
        return base + lax.rem(seat + d, PLANE)

    def at_y(dy):
        return lax.rem(row + dy * PLANE + rows_n, rows_n)

    def to_z(src, dst, ss, rs, k):
        return pltpu.make_async_remote_copy(
            src, dst, ss, rs, device_id=(row, at_z(k)), device_id_type=MESH
        )

    def to_row(src, dst, ss, rs, r):
        return pltpu.make_async_remote_copy(src, dst, ss, rs, device_id=(r, me), device_id_type=MESH)

    def whole_set(buf, count, ss, rs):
        part = buf.at[pl.ds(0, count)]
        return to_z(part, part, ss, rs, 1)

    def all_in(buf, count, n):
        whole_set(buf, count, send_sem.at[n], recv_sem.at[n]).wait_recv()

    def all_out(buf, count, n):
        whole_set(buf, count, send_sem.at[n], recv_sem.at[n]).wait_send()

    barrier = pltpu.get_barrier_semaphore()

    @pl.loop(1, ZN)
    def _(k):
        pl.semaphore_signal(barrier, inc=1, device_id=(row, at_z(k)), device_id_type=MESH)
        pl.semaphore_signal(barrier, inc=1, device_id=(at_seat(k), me), device_id_type=MESH)

    for dy in (1, -1):
        pl.semaphore_signal(barrier, inc=1, device_id=(at_y(dy), me), device_id_type=MESH)

    xin = (xin_a, xin_b)
    packed_buf = (packed_a, packed_b)
    delta_send = (delta_send_a, delta_send_b)
    delta_buf = (delta_buf_a, delta_buf_b)
    q_send = (q_send_a, q_send_b)
    q_buf = (q_buf_a, q_buf_b)
    o_send = (o_send_a, o_send_b)
    a_buf = (a_buf_a, a_buf_b)

    def cells_of(z, part):
        first, rows = PARTS[part]
        return fact_hbm.at[pl.ds(6 * z + first, rows)]

    tile_in = pltpu.make_async_copy(tile_hbm, tile_ref, in_sem.at[0])
    xin_in = [
        pltpu.make_async_copy(cells_of(me, part), xin[part].at[me], in_sem.at[6 * part + 1])
        for part in range(2)
    ]
    gain_in = pltpu.make_async_copy(gain_col_hbm, gain_col_ref, in_sem.at[2])
    gain2_in = pltpu.make_async_copy(gain_tile_hbm, gain_tile_ref, in_sem.at[3])
    mask_in = pltpu.make_async_copy(mask_hbm, mask_ref, in_sem.at[4])
    fact_in = pltpu.make_async_copy(fact_hbm, fact_ref, in_sem.at[5])
    w_copies = [
        pltpu.make_async_copy(w_qkv_hbm, w_qkv, w_sem.at[0]),
        pltpu.make_async_copy(w_col_hbm, w_col, w_sem.at[1]),
        pltpu.make_async_copy(w_query_hbm, w_query, w_sem.at[2]),
    ] + [
        pltpu.make_async_copy(
            w_out_hbm.at[pl.ds(64 * h, 64)], w_twice.at[pl.ds(64 * n, 64)], w_sem.at[3]
        )
        for n, h in enumerate(h for h in range(ZN) for _ in range(2))
    ]
    for copy in xin_in + [tile_in, gain_in, gain2_in, mask_in, fact_in] + w_copies:
        copy.start()

    lane8 = lax.broadcasted_iota(jnp.int32, (8, 128), 1)
    picks = jnp.zeros((8, 128), jnp.int32)
    order = jnp.zeros((8, 128), jnp.int32)
    y_me = row >> 3
    slots = []
    for j in range(maxt):
        slot_id = ids_ref[0, j]
        picks = jnp.where(lane8 == (slot_id >> 2), slot_id & 3, picks)
        owner = jnp.where(slot_id >= 0, slot_id >> 2, row)
        dy = (y_me - (owner >> 3)) & 7
        step = jnp.where(dy <= 4, jnp.maximum(2 * dy - 1, 0), 2 * (8 - dy))
        slots.append((step * 8 + (owner & 7), (step < EARLY_STEPS).astype(jnp.int32)))
    n_early = sum(early for _, early in slots)
    seen = jnp.int32(0)
    for j, (spot, early) in enumerate(slots):
        rank = jnp.where(early > 0, seen, n_early + (j - seen))
        order = jnp.where(lane8 == rank, spot * 64 + j, order)
        seen = seen + early
    my_list[...] = picks
    lists[0] = picks
    lists[PLANE] = order
    pl.semaphore_wait(barrier, 16)

    def cell_copy(k, part):
        return to_z(
            cells_of(at_z(k), part), xin[part].at[me], send_sem.at[part], recv_sem.at[part], k
        )

    def list_copy(k):
        return to_row(my_list, lists.at[k], send_sem.at[2], recv_sem.at[2], at_seat(k))

    for part in range(2):

        @pl.loop(1, ZN)
        def _(k):
            cell_copy(k, part).start()

    @pl.loop(1, PLANE)
    def _(k):
        list_copy(k).start()

    y_bufs = (None, y1, y2, y3, y4, y5, y6, y7)

    def y_forward(src, number, sign, half):
        part = pl.ds(2 * half, 2)
        to_row(
            src.at[part],
            y_bufs[number + 1].at[part],
            send_sem.at[4],
            y_sem.at[number, half],
            at_y(sign),
        ).start()

    for half in range(2):
        y_forward(tile_hbm, 0, 1, half)
        y_forward(tile_hbm, 4, -1, half)

    for k in range(1, 4):
        to_row(
            tile_hbm, x_row.at[k - 1], send_sem.at[3], recv_sem.at[3], at_seat(2 * k)
        ).start()

    def spot_of(s):
        if s < EARLY_STEPS:
            return kv_early.at[s * PLANE + seat]
        return kv_late.at[(s - EARLY_STEPS) * PLANE + seat]

    def x_copy(s, d):
        n = 5 if s < EARLY_STEPS else 6
        return to_row(
            x_send.at[s - 1, d - 1], spot_of(s), send_sem.at[n], recv_sem.at[n], at_seat(d)
        )

    def hand_out(s):
        dy, number = STEPS[s]
        src = y_bufs[number]
        owner = at_y(-dy)
        spot_of(s)[...] = src[lists_s[0, 0, owner]]

        @pl.loop(1, PLANE)
        def _(d):
            x_send[s - 1, d - 1] = src[lists_s[PLANE - d, 0, owner]]
            x_copy(s, d).start()

    def hand_out_row():
        core = row & 1
        for k in range(4):
            src = x_row.at[k - 1] if k else tile_ref
            owner = at_seat(PLANE - 2 * k)
            spot = kv_early.at[owner - base]
            spot[...] = src[lists_s[0, 0, owner]]
            x_sib[k] = src[lists_s[7 - 6 * core, 0, owner]]
            to_row(
                x_sib.at[k], spot, send_sem.at[5], recv_sem.at[5], row + 1 - 2 * core
            ).start()

    def relay(steps):
        for half in range(2):
            part = pl.ds(2 * half, 2)
            for s in steps:
                dy, number = STEPS[s]
                buf = y_bufs[number].at[part]
                sem = number - 1
                to_row(buf, buf, send_sem.at[4], y_sem.at[sem, half], at_y(1)).wait_recv()
                if 0 < dy < 4:
                    y_forward(y_bufs[number], number, 1, half)
                if -3 < dy < 0:
                    y_forward(y_bufs[number], number, -1, half)

    relay((1, 2))
    all_in(lists, PLANE - 1, 2)
    to_smem = pltpu.make_async_copy(lists, lists_s, list_sem)
    to_smem.start()
    to_smem.wait()
    hand_out(1)
    hand_out(2)

    def q_copy(k, part):
        return to_z(
            q_send[part].at[at_z(k)],
            q_buf[part].at[me],
            send_sem.at[8 + part],
            recv_sem.at[8 + part],
            k,
        )

    def delta_copy(k, part):
        return to_z(
            delta_send[part].at[at_z(k)],
            delta_buf[part].at[me],
            send_sem.at[10 + part],
            recv_sem.at[10 + part],
            k,
        )

    gain_in.wait()
    for part, (_, rows) in enumerate(PARTS):
        cells = ZN * 4 * rows
        all_in(xin[part], ZN - 1, part)
        xin_in[part].wait()
        x = xin[part][...].astype(F32).reshape(cells, D)
        normed = rms(x, gain_col_ref[...])
        if part == 0:
            w_copies[0].wait()
        packed = packed_buf[part]
        packed[...] = jnp.dot(normed, w_qkv[...], preferred_element_type=F32).astype(BF)

        same_row = row_of((cells, cells), 0, rows) == row_of((cells, cells), 1, rows)
        low = lax.broadcasted_iota(jnp.int32, (cells, 128), 1) < 64
        mixed = []
        for pair in range(4):
            q2 = packed[:, pl.ds(128 * pair, 128)]
            k2 = packed[:, pl.ds(D + 128 * pair, 128)]
            v2 = packed[:, pl.ds(2 * D + 128 * pair, 128)]
            outs = []
            for half in range(2):
                q1 = jnp.where(low if half == 0 else ~low, q2, jnp.zeros_like(q2))
                s = lax.dot_general(q1, k2, NT, preferred_element_type=F32) * 0.125
                s = jnp.where(same_row, s, -1e30)
                e = jnp.exp(s - jnp.max(s, axis=1, keepdims=True))
                w = (e / jnp.sum(e, axis=1, keepdims=True)).astype(BF)
                outs.append(jnp.dot(w, v2, preferred_element_type=F32))
            mixed.append(jnp.where(low, outs[0], outs[1]).astype(BF))
        mixed = jnp.concatenate(mixed, axis=1)
        if part == 0:
            w_copies[1].wait()
        delta = jnp.dot(mixed, w_col[...], preferred_element_type=F32)
        if part == 0:
            gain2_in.wait()
        normed2 = rms(x + delta, gain_tile_ref[...])
        if part == 0:
            w_copies[2].wait()
        asked = jnp.dot(normed2, w_query[...], preferred_element_type=F32)
        asked = asked * (0.125 * math.log2(math.e))
        lower = lax.broadcasted_iota(jnp.int32, (cells // 2, 128), 1) < 64
        for pair in range(4):
            top = asked[: cells // 2, 128 * pair : 128 * pair + 128]
            bot = asked[cells // 2 :, 128 * pair : 128 * pair + 128]
            q_send[part][2 * pair] = jnp.where(lower, top, pltpu.roll(bot, 64, 1)).astype(BF)
            q_send[part][2 * pair + 1] = jnp.where(lower, pltpu.roll(top, 64, 1), bot).astype(BF)
        delta_send[part][...] = delta.reshape(ZN, 4 * rows, D).astype(BF)
        q_buf[part][me] = q_send[part][me]
        delta_buf[part][me] = delta_send[part][me]

        @pl.loop(1, ZN)
        def _(k):
            q_copy(k, part).start()

        if part == 0:
            relay((3, 4))
            hand_out(3)
            hand_out(4)

    tile_in.wait()
    part_in = x_row.at[pl.ds(0, 3)]
    to_z(part_in, part_in, send_sem.at[3], recv_sem.at[3], 1).wait_recv()
    hand_out_row()

    @pl.loop(1, ZN)
    def _(k):
        for part in range(2):
            delta_copy(k, part).start()

    mask_in.wait()
    dead = jnp.where(mask_ref[...] > 0, 0.0, -1e30)
    rows_dev = dead.shape[0]
    dead = jnp.concatenate(
        [jnp.zeros((rows_dev, 64), F32), dead, jnp.zeros((rows_dev, 64 - maxt), F32)], axis=1
    ).astype(BF)
    relay((5, 6))
    hand_out(5)
    hand_out(6)

    @pl.loop(0, ZN)
    def _(z):
        at = 0
        for first, rows in PARTS:
            cells = ZN * 4 * rows
            mine = z * 6 + first + row_of((cells, rows_dev), 0, rows)
            pick = jnp.where(
                lax.broadcasted_iota(jnp.int32, (cells, rows_dev), 1) == mine, 1.0, 0.0
            )
            bias = jnp.dot(pick.astype(BF), dead, preferred_element_type=F32)
            q_all[z, at : at + cells] = bias.astype(BF)
            at += cells

    for part in range(2):
        all_in(q_buf[part], ZN - 1, 8 + part)

    @pl.loop(0, ZN)
    def _(z):
        at = 0
        for part, (_, rows) in enumerate(PARTS):
            half = ZN * 2 * rows
            q = q_buf[part][z].astype(F32)
            lower = lax.broadcasted_iota(jnp.int32, (half, 128), 1) < 64
            for queries in (q, pltpu.roll(q, 64, 1)):
                bias = q_all[z, at : at + half].astype(F32)
                q_all[z, at : at + half] = jnp.where(lower, queries, bias).astype(BF)
                at += half

    relay((7,))
    hand_out(7)

    lane = lax.broadcasted_iota(jnp.int32, (128, 128), 1)

    def place(n, kv, mark, k_ref, v_ref):
        kv = kv.astype(F32)
        at = pl.ds(pl.multiple_of(n * 128, 128), 128)
        k_ref[at, :] = jnp.where(lane < 64, kv, jnp.where(lane == 64 + mark, 1.0, 0.0)).astype(BF)
        v_ref[at, :] = jnp.where(lane < 64, jnp.where(lane == 0, 1.0, 0.0), kv).astype(BF)

    def sweep(k_ref, v_ref, width, finish, earlier):
        def stage(later, s_later, now, s_now, tops):
            found = None
            if later is not None:
                s = lax.dot_general(q_all[later], k_ref[...], NT, preferred_element_type=F32)
                s_later[:, :width] = s
                found = jnp.max(s, axis=1, keepdims=True)
                if earlier:
                    found = jnp.maximum(found, m_first[later, :, 0:1])
            if now is not None:
                p = jnp.exp2(s_now[:, :width] - tops).astype(BF)
                o = jnp.dot(p, v_ref[...], preferred_element_type=F32)
                finish(now, o, tops, s_now is s_odd)
            return found

        def two(i, tops):
            tops = stage(2 * i + 1, s_odd, 2 * i, s_even, tops)
            return stage(2 * i + 2, s_even, 2 * i + 1, s_odd, tops)

        tops = stage(0, s_even, None, None, None)
        tops = lax.fori_loop(0, ZN // 2 - 1, two, tops)
        tops = stage(ZN - 1, s_odd, ZN - 2, s_even, tops)
        stage(None, None, ZN - 1, s_odd, tops)

    all_in(kv_early, (EARLY_STEPS - 1) * (PLANE - 1) + 4, 5)
    @pl.loop(0, EARLY)
    def _(n):
        code = lists_s[PLANE, 0, n]
        spot = jnp.minimum(code >> 6, EARLY_STEPS * PLANE - 1)
        place(n, kv_early[spot], code & 63, k_early, v_early)

    def keep(z, o, tops, odd):
        o_first[z] = o
        m_first[z] = jnp.broadcast_to(tops, (CELLS, 128))

    sweep(k_early, v_early, EARLY * 128, keep, False)

    all_in(kv_late, (8 - EARLY_STEPS) * (PLANE - 1), 6)
    @pl.loop(EARLY, maxt)
    def _(n):
        code = lists_s[PLANE, 0, n]
        spot = code >> 6
        first = kv_early[jnp.minimum(spot, EARLY_STEPS * PLANE - 1)].astype(F32)
        second = kv_late[jnp.maximum(spot - EARLY_STEPS * PLANE, 0)].astype(F32)
        place(
            n - EARLY,
            jnp.where(spot < EARLY_STEPS * PLANE, first, second),
            code & 63,
            k_late,
            v_late,
        )

    def o_copy(pair, k, part):
        n = 12 + 2 * (pair >= LAST) + part
        return to_z(
            o_send[part].at[pair, at_z(k)],
            a_buf[part].at[pair, me],
            send_sem.at[12 + part],
            recv_sem.at[n],
            k,
        )

    def send(z, o, tops, odd):
        o = o + o_first[z] * jnp.exp2(m_first[z, :, 0:1] - tops)
        o = o / o[:, 0:1]
        if not odd:
            o_even[...] = pltpu.roll(o, 64, 1)
            return
        low = lax.broadcasted_iota(jnp.int32, (CELLS, 128), 1) < 64
        o = jnp.where(low, o_even[...], o)
        pair = z // 2 if isinstance(z, int) else z >> 1
        at = 0
        for part, (_, rows) in enumerate(PARTS):
            cells = ZN * 4 * rows
            o_send[part][pair] = o[at : at + cells].reshape(ZN, 4 * rows, 128).astype(BF)
            a_buf[part][pair, me] = o_send[part][pair, me]
            at += cells

        @pl.loop(1, ZN)
        def _(k):
            for part in range(2):
                o_copy(pair, k, part).start()

    sweep(k_late, v_late, (maxt - EARLY) * 128, send, True)

    pltpu.make_async_copy(w_twice, w_twice, w_sem.at[3]).wait()
    fact_in.wait()

    for part in range(2):
        all_in(delta_buf[part], ZN - 1, 10 + part)
    def joined(bufs):
        both = jnp.concatenate([buf.astype(F32) for buf in bufs], axis=1)
        return both.reshape(both.shape[0] * GROUP, both.shape[2])

    for first, last, n in ((0, LAST, 12), (LAST, ZN // 2, 14)):
        for part in range(2):
            came = a_buf[part].at[pl.ds(first, last - first), pl.ds(0, ZN - 1)]
            to_z(came, came, send_sem.at[12 + part], recv_sem.at[n + part], 1).wait_recv()
        pairs = last - first
        cells = pairs * GROUP
        low = lax.broadcasted_iota(jnp.int32, (cells, 128), 1) < 64
        heads = [joined([a_buf[part][first:last, h] for part in range(2)]) for h in range(ZN)]
        base_rows = fact_ref[12 * first : 12 * last].astype(F32).reshape(2 * cells, D)
        more = joined([delta_buf[part][2 * first : 2 * last] for part in range(2)])
        answer = jnp.concatenate(
            [
                jnp.concatenate([jnp.where(side, a, 0.0).astype(BF) for a in heads], axis=1)
                for side in (low, ~low)
            ],
            axis=0,
        )
        got = jnp.dot(answer, w_twice[...], preferred_element_type=F32)
        got = jnp.concatenate(
            [
                got[side * cells + GROUP * n : side * cells + GROUP * (n + 1)]
                for n in range(pairs)
                for side in range(2)
            ],
            axis=0,
        )
        final = base_rows + more + got
        out_ref[12 * first : 12 * last] = final.reshape(12 * pairs, 4, D).astype(BF)

    for part in range(2):
        all_out(xin[part], ZN - 1, part)
        all_out(q_send[part], ZN - 1, 8 + part)
        all_out(delta_send[part], ZN - 1, 10 + part)
        out = o_send[part].at[pl.ds(0, ZN // 2), pl.ds(0, ZN - 1)]
        to_z(out, out, send_sem.at[12 + part], recv_sem.at[12 + part], 1).wait_send()
    all_out(lists, PLANE - 1, 2)
    all_out(x_row, 3, 3)
    all_out(kv_early, 4 * 7, 4)
    all_out(kv_early, (EARLY_STEPS - 1) * (PLANE - 1) + 4, 5)
    all_out(kv_late, (8 - EARLY_STEPS) * (PLANE - 1), 6)


def shards(
    fact_cells,
    gain_col,
    w_qkv,
    w_col_out,
    gain_tile,
    w_query,
    w_tile_out,
    tile_kv,
    tile_ids,
    key_mask,
    *,
    rows_n,
):
    maxt = tile_ids.shape[1]
    vmem = pl.BlockSpec(memory_space=pltpu.VMEM)
    smem = pl.BlockSpec(memory_space=pltpu.SMEM)
    anywhere = pl.BlockSpec(memory_space=pl.ANY)
    tiles = tile_kv.reshape(tile_kv.shape[0], tile_kv.shape[1], tile_kv.shape[3])
    dma = pltpu.SemaphoreType.DMA
    return pl.pallas_call(
        functools.partial(layer_kernel, rows_n, maxt),
        out_shape=jax.ShapeDtypeStruct(fact_cells.shape, BF),
        in_specs=[smem] + [anywhere] * 9,
        out_specs=vmem,
        scratch_shapes=[
            pltpu.VMEM(key_mask.shape, jnp.int32),
            pltpu.VMEM(fact_cells.shape, BF),
            pltpu.VMEM((1, D), F32),
            pltpu.VMEM((1, D), F32),
            pltpu.VMEM(tiles.shape, BF),
            pltpu.VMEM((ZN, PARTS[0][1], 4, D), BF),
            pltpu.VMEM((ZN, PARTS[1][1], 4, D), BF),
            pltpu.VMEM((ZN * 4 * PARTS[0][1], 3 * D), BF),
            pltpu.VMEM((ZN * 4 * PARTS[1][1], 3 * D), BF),
        ]
        + [pltpu.VMEM((ZN, 4 * rows, D), BF) for _ in range(2) for _, rows in PARTS]
        + [pltpu.VMEM((ZN, ZN * 2 * rows, 128), BF) for _ in range(2) for _, rows in PARTS]
        + [pltpu.VMEM((ZN, CELLS, 128), BF)]
        + [pltpu.VMEM((ZN // 2, ZN, 4 * rows, 128), BF) for _ in range(2) for _, rows in PARTS]
        + [
            pltpu.VMEM((3,) + tiles.shape, BF),
            pltpu.VMEM((4, 128, 128), BF),
        ]
        + [pltpu.VMEM(tiles.shape, BF)] * 7
        + [
            pltpu.VMEM((7, PLANE - 1, 128, 128), BF),
            pltpu.VMEM((EARLY_STEPS * PLANE, 128, 128), BF),
            pltpu.VMEM(((8 - EARLY_STEPS) * PLANE, 128, 128), BF),
            pltpu.VMEM((EARLY * 128, 128), BF),
            pltpu.VMEM((EARLY * 128, 128), BF),
            pltpu.VMEM(((maxt - EARLY) * 128, 128), BF),
            pltpu.VMEM(((maxt - EARLY) * 128, 128), BF),
            pltpu.VMEM((CELLS, EARLY * 128), F32),
            pltpu.VMEM((CELLS, EARLY * 128), F32),
            pltpu.VMEM((ZN, CELLS, 128), F32),
            pltpu.VMEM((ZN, CELLS, 128), F32),
            pltpu.VMEM((CELLS, 128), F32),
            pltpu.VMEM((8, 128), jnp.int32),
            pltpu.VMEM((PLANE + 1, 8, 128), jnp.int32),
            pltpu.SMEM((PLANE + 1, 8, 128), jnp.int32),
            pltpu.VMEM((D, 3 * D), BF),
            pltpu.VMEM((D, D), BF),
            pltpu.VMEM((D, D), BF),
            pltpu.VMEM((2 * D, D), BF),
            dma((8,)),
            dma((4,)),
            dma,
            dma((7, 2)),
            dma((14,)),
            dma((16,)),
        ],
        compiler_params=pltpu.CompilerParams(
            collective_id=0, has_side_effects=True, vmem_limit_bytes=60 << 20
        ),
    )(
        tile_ids,
        key_mask,
        fact_cells,
        gain_col.reshape(1, D),
        gain_tile.reshape(1, D),
        tiles,
        w_qkv,
        w_col_out,
        w_query,
        w_tile_out,
    )


def solution(mesh):
    placed = (
        P("rows", "cols", None),
        P(),
        P(),
        P(),
        P(),
        P(),
        P(),
        P("rows", None, "cols", None),
        P("rows", None),
        P("rows", None),
    )
    return jax.shard_map(
        functools.partial(shards, rows_n=mesh.shape["rows"]),
        mesh=mesh,
        in_specs=placed,
        out_specs=P("rows", "cols", None),
        check_vma=False,
    )
```

time: 200 us -> 60.2 us (0.30)
  Pallas kernels: 0 us -> 58.3 us
  waiting for transfers between devices: 52.6 us -> 0 us
  matrix products: 34.6 us -> 0 us
  blocking collectives: 27.9 us -> 0 us
  local copies, waits for them, and re-layouts: 27.5 us -> 1.67 us
  other arithmetic: 23.4 us -> 0 us
  starting transfers between devices: 17.9 us -> 0 us
  between operations: 13.8 us -> 0.01 us
    pallas_call x0 -> x1, Pallas kernels: none -> 58.3 us  [shards(): pl.pallas_call(functools.partial(layer_kernel, rows_n, maxt), out_shape=j...]
    dot_general x29 -> x0, matrix products: 33.2 us -> none  [the longest x12 17.6 us: one_block(): jnp.einsum('rchd,tkhd->rchtk', block_q, key_part, preferred_element_type=...]
    all_to_all x2 -> x0, blocking collectives: 27.9 us -> none  [the longest x1 16.5 us: shards(): lax.all_to_all(answer, 'cols', split_axis=1, concat_axis=2, tiled=True)]
    all_to_all x3 -> x0, waiting for transfers between devices: 26.6 us -> none  [the longest x1 11.1 us: shards(): lax.all_to_all(keyvals, 'cols', split_axis=2, concat_axis=1, tiled=True)]
    all_gather x1 -> x0, waiting for transfers between devices: 25.3 us -> none  [fetch_all(): gathered = lax.all_gather(tile_kv, 'rows', axis=0, tiled=True)]
    all_to_all x3 -> x0, starting transfers between devices: 17.9 us -> none  [the longest x1 10.9 us: shards(): lax.all_to_all(queries, 'cols', split_axis=2, concat_axis=1, tiled=True)]
    reduce_sum x13 -> x0, other arithmetic: 12.4 us -> none  [the longest x12 11.4 us: soft_weights(): jnp.sum(expo_vals, axis=axes, keepdims=True)]
    gt x12 -> x0, other arithmetic: 8.23 us -> none  [one_block(): live_keys = (block_m > 0)[:, None, None, :, None]]
  transfers between devices with their start and end apart: 4 -> 0, of which waited for: 4 -> 0; matrix products, arithmetic and copies ran while one was open for 8% -> 0% of each run, Pallas kernels for 0% -> 0%
where the time goes in v2:
time: 60.2 us; the launch traced here: 60 us
  Pallas kernels  58.3 us (97%)
  local copies, waits for them, and re-layouts  1.67 us (3%)
    pallas_call x1, Pallas kernels, shards(): pl.pallas_call(functools.partial(layer_kernel, rows_n, maxt), out_shape=j...  58.3 us
    unnamed x1, local copies, waits for them, and re-layouts  1.67 us

profile of v2, /device:TPU:1, one launch (start us, length us, event | category | flops | bytes accessed | tf_op | source)
XLA Modules:
  0.0 60.0 jit_solution(8017465005150431591)
XLA Ops:
  0.0 58.3 %shard_map.100 = bf16[48,4,512]{2,1,0:T(4,128)(2,1)} custom-call(s32[1,48]{1,0:T(1,128)} %ids_ref.1, s32[48,48]{1,0:T(8,128)} %mask_hbm.1, bf16[48,4,512]{2,1,0:T(4,128)(2,1)} %fact_hbm.1, f32[1,512]{1,0:T(1,128)} %bitcast.4, f32[1,512]{1,0:T(1,128)} %bitcast.5, bf16[4,128,128]{2,1,0:T(8,128)(2,1)} %bitcast.3, bf16[512,1536]{1,0:T(8,128)(2,1)} %w_qkv_hbm.1, ...), custom_call_target="tpu_custom_call" | custom-call | tf_op jit(solution)/shard_map/pallas_call | solution.py:590
  58.4 1.7 %copy.12 = bf16[48,4,512]{2,1,0:T(4,128)(2,1)} copy(bf16[48,4,512]{2,1,0:T(4,128)(2,1)} %shard_map.100) | data formatting | bytes 393216

commit v3 on v2

--- a/solution.py
+++ b/solution.py
@@ -15,7 +15,7 @@
 GROUP = 24
 CELLS = ZN * GROUP
 D = 512
-EARLY_STEPS, EARLY = 6, 32
+EARLY_STEPS, EARLY = 5, 24
 PARTS = ((0, 4), (4, 2))
 LAST = 3
 PLANE = 8
@@ -288,10 +288,10 @@
                 if -3 < dy < 0:
                     y_forward(y_bufs[number], number, -1, half)
 
-    relay((1, 2))
     all_in(lists, PLANE - 1, 2)
     to_smem = pltpu.make_async_copy(lists, lists_s, list_sem)
     to_smem.start()
+    relay((1, 2))
     to_smem.wait()
     hand_out(1)
     hand_out(2)
@@ -325,6 +325,10 @@
             w_copies[0].wait()
         packed = packed_buf[part]
         packed[...] = jnp.dot(normed, w_qkv[...], preferred_element_type=F32).astype(BF)
+        if part == 1:
+            relay((3, 4))
+            hand_out(3)
+            hand_out(4)
 
         same_row = row_of((cells, cells), 0, rows) == row_of((cells, cells), 1, rows)
         low = lax.broadcasted_iota(jnp.int32, (cells, 128), 1) < 64
@@ -366,11 +370,6 @@
         @pl.loop(1, ZN)
         def _(k):
             q_copy(k, part).start()
-
-        if part == 0:
-            relay((3, 4))
-            hand_out(3)
-            hand_out(4)
 
     tile_in.wait()
     part_in = x_row.at[pl.ds(0, 3)]

time: 60.2 us -> 56.4 us (0.937)
  Pallas kernels: 58.3 us -> 54.5 us
    pallas_call x1, Pallas kernels: 58.3 us -> 54.5 us  [shards(): pl.pallas_call(functools.partial(layer_kernel, rows_n, maxt), out_shape=j...]
where the time goes in v3:
time: 56.4 us; the launch traced here: 56.2 us
  Pallas kernels  54.5 us (97%)
  local copies, waits for them, and re-layouts  1.67 us (3%)
    pallas_call x1, Pallas kernels, shards(): pl.pallas_call(functools.partial(layer_kernel, rows_n, maxt), out_shape=j...  54.5 us
    unnamed x1, local copies, waits for them, and re-layouts  1.67 us

profile of v3, /device:TPU:1, one launch (start us, length us, event | category | flops | bytes accessed | tf_op | source)
XLA Modules:
  0.0 56.2 jit_solution(5972041482640907124)
XLA Ops:
  0.0 54.5 %shard_map.100 = bf16[48,4,512]{2,1,0:T(4,128)(2,1)} custom-call(s32[1,48]{1,0:T(1,128)} %ids_ref.1, s32[48,48]{1,0:T(8,128)} %mask_hbm.1, bf16[48,4,512]{2,1,0:T(4,128)(2,1)} %fact_hbm.1, f32[1,512]{1,0:T(1,128)} %bitcast.4, f32[1,512]{1,0:T(1,128)} %bitcast.5, bf16[4,128,128]{2,1,0:T(8,128)(2,1)} %bitcast.3, bf16[512,1536]{1,0:T(8,128)(2,1)} %w_qkv_hbm.1, ...), custom_call_target="tpu_custom_call" | custom-call | tf_op jit(solution)/shard_map/pallas_call | solution.py:589
  54.5 1.7 %copy.12 = bf16[48,4,512]{2,1,0:T(4,128)(2,1)} copy(bf16[48,4,512]{2,1,0:T(4,128)(2,1)} %shard_map.100) | data formatting | bytes 393216

commit v4 on v3

--- a/solution.py
+++ b/solution.py
@@ -376,11 +376,6 @@
     to_z(part_in, part_in, send_sem.at[3], recv_sem.at[3], 1).wait_recv()
     hand_out_row()
 
-    @pl.loop(1, ZN)
-    def _(k):
-        for part in range(2):
-            delta_copy(k, part).start()
-
     mask_in.wait()
     dead = jnp.where(mask_ref[...] > 0, 0.0, -1e30)
     rows_dev = dead.shape[0]
@@ -404,8 +399,31 @@
             q_all[z, at : at + cells] = bias.astype(BF)
             at += cells
 
+    lane = lax.broadcasted_iota(jnp.int32, (128, 128), 1)
+
+    def place(n, kv, mark, k_ref, v_ref):
+        kv = kv.astype(F32)
+        at = pl.ds(pl.multiple_of(n * 128, 128), 128)
+        k_ref[at, :] = jnp.where(lane < 64, kv, jnp.where(lane == 64 + mark, 1.0, 0.0)).astype(BF)
+        v_ref[at, :] = jnp.where(lane < 64, jnp.where(lane == 0, 1.0, 0.0), kv).astype(BF)
+
+    all_in(kv_early, (EARLY_STEPS - 1) * (PLANE - 1) + 4, 5)
+    @pl.loop(0, EARLY)
+    def _(n):
+        code = lists_s[PLANE, 0, n]
+        spot = jnp.minimum(code >> 6, EARLY_STEPS * PLANE - 1)
+        place(n, kv_early[spot], code & 63, k_early, v_early)
+
+    relay((7,))
+    hand_out(7)
+
     for part in range(2):
         all_in(q_buf[part], ZN - 1, 8 + part)
+
+    @pl.loop(1, ZN)
+    def _(k):
+        for part in range(2):
+            delta_copy(k, part).start()
 
     @pl.loop(0, ZN)
     def _(z):
@@ -418,17 +436,6 @@
                 bias = q_all[z, at : at + half].astype(F32)
                 q_all[z, at : at + half] = jnp.where(lower, queries, bias).astype(BF)
                 at += half
-
-    relay((7,))
-    hand_out(7)
-
-    lane = lax.broadcasted_iota(jnp.int32, (128, 128), 1)
-
-    def place(n, kv, mark, k_ref, v_ref):
-        kv = kv.astype(F32)
-        at = pl.ds(pl.multiple_of(n * 128, 128), 128)
-        k_ref[at, :] = jnp.where(lane < 64, kv, jnp.where(lane == 64 + mark, 1.0, 0.0)).astype(BF)
-        v_ref[at, :] = jnp.where(lane < 64, jnp.where(lane == 0, 1.0, 0.0), kv).astype(BF)
 
     def sweep(k_ref, v_ref, width, finish, earlier):
         def stage(later, s_later, now, s_now, tops):
@@ -453,13 +460,6 @@
         tops = lax.fori_loop(0, ZN // 2 - 1, two, tops)
         tops = stage(ZN - 1, s_odd, ZN - 2, s_even, tops)
         stage(None, None, ZN - 1, s_odd, tops)
-
-    all_in(kv_early, (EARLY_STEPS - 1) * (PLANE - 1) + 4, 5)
-    @pl.loop(0, EARLY)
-    def _(n):
-        code = lists_s[PLANE, 0, n]
-        spot = jnp.minimum(code >> 6, EARLY_STEPS * PLANE - 1)
-        place(n, kv_early[spot], code & 63, k_early, v_early)
 
     def keep(z, o, tops, odd):
         o_first[z] = o

time: 56.4 us -> 56.7 us (level)
  no operation moved by 1% of the time
where the time goes in v4:
time: 56.7 us; the launch traced here: 56.6 us
  Pallas kernels  54.9 us (97%)
  local copies, waits for them, and re-layouts  1.67 us (3%)
    pallas_call x1, Pallas kernels, shards(): pl.pallas_call(functools.partial(layer_kernel, rows_n, maxt), out_shape=j...  54.9 us
    unnamed x1, local copies, waits for them, and re-layouts  1.67 us

profile of v4, /device:TPU:1, one launch (start us, length us, event | category | flops | bytes accessed | tf_op | source)
XLA Modules:
  0.0 56.6 jit_solution(11782315412152646639)
XLA Ops:
  0.0 54.9 %shard_map.100 = bf16[48,4,512]{2,1,0:T(4,128)(2,1)} custom-call(s32[1,48]{1,0:T(1,128)} %ids_ref.1, s32[48,48]{1,0:T(8,128)} %mask_hbm.1, bf16[48,4,512]{2,1,0:T(4,128)(2,1)} %fact_hbm.1, f32[1,512]{1,0:T(1,128)} %bitcast.4, f32[1,512]{1,0:T(1,128)} %bitcast.5, bf16[4,128,128]{2,1,0:T(8,128)(2,1)} %bitcast.3, bf16[512,1536]{1,0:T(8,128)(2,1)} %w_qkv_hbm.1, ...), custom_call_target="tpu_custom_call" | custom-call | tf_op jit(solution)/shard_map/pallas_call | solution.py:589
  54.9 1.7 %copy.12 = bf16[48,4,512]{2,1,0:T(4,128)(2,1)} copy(bf16[48,4,512]{2,1,0:T(4,128)(2,1)} %shard_map.100) | data formatting | bytes 393216
